TPU v7x, 32 devices: a whole 2x2x4 slice. The times are simulated.
32 devices in a mesh: dp: 4 (over y, x), mp: 8 (over z, core).
Axes of the slice: x: 2, y: 2, z: 4, core: 2. Of those that a mesh axis runs over, the one named last changes fastest.
Arguments:
- grads: bfloat16 [3, 8192, 28672], P(None, 'dp', 'mp'), may hold values from -8 to 8
- sketch: bfloat16 [28672, 256], P('mp'), may hold values from -0.03125 to 0.03125
- old_proj: bfloat16 [3, 8192, 256], P(None, 'dp'), may hold values from -0.0625 to 0.0625
- first_moment: float32 [3, 256, 28672], P(None, 'dp', 'mp'), may hold values from -12 to 12
- second_moment: float32 [3, 256, 28672], P(None, 'dp', 'mp'), may hold values from 0.25 to 4
- refresh_list: int32 [1], replicated, may hold values from 0 to 2
Outputs:
- new_first: float32 [3, 256, 28672], P(None, 'dp', 'mp')
- new_second: float32 [3, 256, 28672], P(None, 'dp', 'mp')
- direction: bfloat16 [3, 256, 28672], P(None, 'dp', 'mp')
All inputs are finite; a program needn't handle non-finite values.
Results may differ from a plain program's by a relative error of at most 0.0029.
Values sent between devices are 32-bit elements; how exact they have to be, the bound alone decides.
No kernel may reach another device: no remote copies, remote signals or barrier semaphores. Data moves between devices by JAX's collectives and lax.ppermute only.
A program may use at most 192 MiB of HBM per device.

v0:
```python
import jax
import jax.numpy as jnp
from jax import lax
from jax.sharding import PartitionSpec as P

first_decay = 0.9
second_decay = 0.95
epsilon = 1e-08
highest = lax.Precision.HIGHEST


def row_product(left, right):
    return lax.dot_general(
        left, right, (((0,), (0,)), ((), ())), precision=highest, preferred_element_type=jnp.float32
    )


def local(grads, sketch, old_proj, first_moment, second_moment, refresh_list):
    chosen = refresh_list[0]
    matrix_count = grads.shape[0]
    rank_rows = first_moment.shape[1]
    rank_total = sketch.shape[1]
    columns_total = sketch.shape[0] * lax.axis_size("mp")
    target = lax.dynamic_index_in_dim(grads, chosen, 0, keepdims=False)
    prior_proj = lax.dynamic_index_in_dim(old_proj, chosen, 0, keepdims=False).astype(jnp.float32)
    sketch_part = jnp.dot(target, sketch, preferred_element_type=jnp.float32)
    sketched = (lax.psum(sketch_part, "mp") / rank_total).astype(jnp.bfloat16)
    backward_part = lax.dot_general(
        target, sketched, (((0,), (0,)), ((), ())), preferred_element_type=jnp.float32
    )
    backward = (lax.psum(backward_part, "dp") / columns_total).astype(jnp.bfloat16)
    range_panel = lax.psum(jnp.dot(target, backward, preferred_element_type=jnp.float32), "mp")
    gram_part = row_product(range_panel, range_panel)
    gram_full = lax.psum(gram_part, "dp")
    factor = jnp.linalg.cholesky(gram_full)
    new_basis = jax.scipy.linalg.solve_triangular(factor, range_panel.T, lower=True).T
    turning = lax.psum(row_product(new_basis, prior_proj), "dp")
    picks = lax.broadcasted_iota(jnp.int32, (matrix_count, 1, 1), 0) == chosen
    projectors = jnp.where(picks, new_basis.astype(jnp.bfloat16)[None], old_proj)
    projected = jnp.transpose(
        lax.psum_scatter(
            jnp.einsum("kdr,kdc->rkc", projectors, grads, preferred_element_type=jnp.float32),
            "dp",
            scatter_dimension=0,
            tiled=True,
        ),
        (1, 0, 2),
    )
    first_own = lax.dynamic_index_in_dim(first_moment, chosen, 0, keepdims=False)
    second_own = lax.dynamic_index_in_dim(second_moment, chosen, 0, keepdims=False)
    own_start = lax.axis_index("dp") * rank_rows
    first_all, second_all = (
        lax.all_gather(first_own, "dp", axis=0, tiled=True),
        lax.all_gather(second_own, "dp", axis=0, tiled=True),
    )
    own_turning = lax.dynamic_slice_in_dim(turning, own_start, rank_rows, 0)
    turned_first = jnp.dot(own_turning, first_all, precision=highest)
    turned_second = jnp.dot(own_turning * own_turning, second_all, precision=highest)
    moved_first = jnp.where(picks, turned_first[None], first_moment)
    moved_second = jnp.where(picks, turned_second[None], second_moment)
    updated_first = first_decay * moved_first + (1.0 - first_decay) * projected
    updated_second = second_decay * moved_second + (1.0 - second_decay) * projected * projected
    direction = (updated_first / (jnp.sqrt(updated_second) + epsilon)).astype(jnp.bfloat16)
    return (updated_first, updated_second, direction)


def solution(mesh):
    placed = (
        P(None, "dp", "mp"),
        P("mp", None),
        P(None, "dp", None),
        P(None, "dp", "mp"),
        P(None, "dp", "mp"),
        P(),
    )
    return jax.shard_map(
        local,
        mesh=mesh,
        in_specs=placed,
        out_specs=(P(None, "dp", "mp"), P(None, "dp", "mp"), P(None, "dp", "mp")),
        check_vma=False,
    )
```

profile of v0, /device:TPU:0, one launch (start us, length us, event | category | flops | bytes accessed | tf_op | source)
XLA Modules:
  0.0 609.4 jit_solution(3067259670049275815)
XLA Ops:
  8.7 8.6 %fusion.4 = f32[2048,256]{1,0:T(8,128)} fusion(bf16[3584,256]{1,0:T(8,128)(2,1)S(1)} %copy-done, bf16[3,2048,3584]{2,1,0:T(8,128)(2,1)} %param.6, s32[]{:T(128)S(6)} %select_n.27), kind=kOutput, calls=%fused_computation.6 | convolution fusion | flops 3758096384 | bytes 18612228 | tf_op jit(solution)/shard_map/dot_general | solution.py:26
  17.3 68.0 %all-reduce.7.cloned.1.call-done = f32[2048,256]{1,0:T(8,128)} async-done(((f32[2048,256]{1,0:T(8,128)}), f32[2048,256]{1,0:T(8,128)}) %all-reduce.7.cloned.1.call-update) | async-done | bytes 2097168 | tf_op jit(solution)/shard_map/psum | solution.py:27
  85.3 11.6 %fusion.2 = f32[3584,256]{1,0:T(8,128)} fusion(bf16[3,2048,3584]{2,1,0:T(8,128)(2,1)} %param.6, s32[]{:T(128)S(6)} %select_n.27, f32[2048,256]{1,0:T(8,128)} %all-reduce.7.cloned.1.call-done), kind=kOutput, calls=%fused_computation.4 | convolution fusion | flops 3759144960 | bytes 20447236 | tf_op jit(solution)/shard_map/dot_general | solution.py:28
  97.0 95.4 %all-reduce.9.cloned.1.call-done = f32[3584,256]{1,0:T(8,128)} async-done(((f32[3584,256]{1,0:T(8,128)}), f32[3584,256]{1,0:T(8,128)}) %all-reduce.9.cloned.1.call-update) | async-done | bytes 3670032 | tf_op jit(solution)/shard_map/psum | solution.py:31
  192.4 11.5 %fusion = f32[2048,256]{1,0:T(8,128)} fusion(bf16[3,2048,3584]{2,1,0:T(8,128)(2,1)} %param.6, s32[]{:T(128)S(6)} %select_n.27, f32[3584,256]{1,0:T(8,128)} %all-reduce.9.cloned.1.call-done), kind=kOutput, calls=%fused_computation.2 | convolution fusion | flops 3759931392 | bytes 20447236 | tf_op jit(solution)/shard_map/dot_general | solution.py:32
  204.4 64.7 %all-reduce.11.cloned.1.call-done = f32[2048,256]{1,0:T(8,128)} async-done(((f32[2048,256]{1,0:T(8,128)}), f32[2048,256]{1,0:T(8,128)}) %all-reduce.11.cloned.1.call-update) | async-done | bytes 2097168 | tf_op jit(solution)/shard_map/psum | solution.py:32
  269.2 6.4 %fusion.48 = f32[256,256]{0,1:T(8,128)} fusion(f32[2048,256]{1,0:T(8,128)} %all-reduce.11.cloned.1.call-done), kind=kOutput, calls=%fused_computation.75 | convolution fusion | flops 1610612736 | bytes 2359296 | tf_op jit(solution)/shard_map/dot_general | solution.py:13
  275.6 2.2 constant_dynamic-slice_fusion.1
  277.9 40.5 %all-reduce.13.cloned.1.call-done = f32[256,256]{0,1:T(8,128)} async-done(((f32[256,256]{0,1:T(8,128)}), f32[256,256]{0,1:T(8,128)}) %all-reduce.13.cloned.1.call-update) | async-done | bytes 262160 | tf_op jit(solution)/shard_map/psum | solution.py:34
  318.4 1.1 copy.10
  319.5 1.0 fusion.27
  320.5 11.7 %cholesky.50 = f32[128,128]{1,0:T(8,128)S(1)} custom-call(f32[128,128]{1,0:T(8,128)S(1)} %cholesky.118), custom_call_target="Cholesky" | custom-call | tf_op jit(solution)/shard_map/jit(cholesky)/cholesky | solution.py:35
  332.2 9.8 %custom-call.15 = f32[1,128,128]{1,2,0:T(8,128)S(1)} custom-call(f32[1,128,128]{2,1,0:T(8,128)S(1)} %get-tuple-element.27), custom_call_target="InvertDiagBlocksLowerTriangular" | custom-call | tf_op jit(solution)/shard_map/jit(cholesky)/cholesky | solution.py:35
  342.5 11.7 %cholesky.105 = f32[128,128]{1,0:T(8,128)S(1)} custom-call(f32[128,128]{1,0:T(8,128)S(1)} %convolution_subtract_fusion.1), custom_call_target="Cholesky" | custom-call | tf_op jit(solution)/shard_map/jit(cholesky)/cholesky | solution.py:35
  356.5 4.2 while.1
  357.2 1.4 bitcast_dynamic-update-slice_fusion.2
  359.3 1.4 bitcast_dynamic-update-slice_fusion.2
  360.7 19.7 %custom-call.16 = f32[2,128,128]{1,2,0:T(8,128)S(1)} custom-call(f32[2,128,128]{2,1,0:T(8,128)S(1)} %get-tuple-element.10), custom_call_target="InvertDiagBlocksLowerTriangular" | custom-call | tf_op jit(solution)/shard_map/jit(_solve_triangular)/triangular_solve | solution.py:36
  380.4 2.3 fusion.22
  382.7 3.0 convolution_subtract_fusion
  385.7 1.1 fusion.29
  386.8 3.0 fusion.19
  389.9 2.2 constant_dynamic-slice_fusion.2
  392.2 1.1 fusion.21
  393.3 1.7 copy.11
  395.0 24.7 %convolution_bitcast_fusion = f32[256,3,3584]{2,0,1:T(8,128)} fusion(bf16[3,2048,3584]{2,1,0:T(8,128)(2,1)} %param.6, bf16[3,2048,256]{2,1,0:T(8,128)(2,1)} %param.8, pred[3]{0:T(512)(128)(4,1)S(1)} %iota_compare_fusion.3, bf16[2048,256]{1,0:T(8,128)(2,1)S(1)} %copy.11), kind=kOutput, calls=%fused_computation.11 | convolution fusion | flops 11275862016 | bytes 59244548 | tf_op jit(solution)/shard_map/kdr,kdc->rkc/dot_general | solution.py:42
  419.8 13.3 %all-reduce.15.cloned.1.call-done = f32[256,256]{1,0:T(8,128)} async-done(((f32[256,256]{1,0:T(8,128)}), f32[256,256]{1,0:T(8,128)}) %all-reduce.15.cloned.1.call-update) | async-done | bytes 262160 | tf_op jit(solution)/shard_map/psum | solution.py:37
  433.0 4.4 fusion.9
  437.4 46.3 %all-gather.5.cloned.1.call-done = f32[1,256,3584]{2,1,0:T(8,128)} async-done(((f32[1,64,3584]{2,1,0:T(8,128)}), f32[1,256,3584]{2,1,0:T(8,128)}) %all-gather.5.cloned.1.call-update) | async-done | bytes 3670032 | tf_op jit(solution)/shard_map/all_gather | solution.py:53
  483.7 5.3 fusion.11
  489.0 105.6 %reduce-scatter.2.cloned.1.call-done = f32[64,3,3584]{2,0,1:T(8,128)} async-done(((f32[256,3,3584]{2,0,1:T(8,128)}), f32[64,3,3584]{2,0,1:T(8,128)}) %reduce-scatter.2.cloned.1.call-update) | async-done | bytes 2752528 | tf_op jit(solution)/shard_map/reduce_scatter | solution.py:41
  594.6 7.8 %divide_convert_fusion = (bf16[3,64,3584]{2,1,0:T(8,128)(2,1)}, f32[3,64,3584]{2,1,0:T(8,128)}, f32[3,64,3584]{2,1,0:T(8,128)}) fusion(f32[64,3,3584]{2,0,1:T(8,128)} %reduce-scatter.2.cloned.1.call-done, f32[3,64,3584]{2,1,0:T(8,128)} %param.10, f32[64,3584]{1,0:T(8,128)S(1)} %fusion.9, pred[3]{0:T(512)(128)(4,1)S(1)} %iota_compare_fusion.3, ...), kind=kLoop, calls=%fused_computation.23 | loop fusion | flops 8257536 | bytes 16973828 | tf_op jit(solution)/shard_map/convert_element_type | solution.py:63
  (37 shorter events, 4.2 us)
Async XLA Ops:
  7.2 1.5 copy-start
  7.2 78.1 %all-reduce.7.cloned.1.call-start = ((), (), s32[]{:S(2)}) async-start(), calls=%async_computation.1 | async-start | bytes 4194304 | tf_op jit(solution)/shard_map/psum | solution.py:27
  17.3 175.1 %all-reduce.9.cloned.1.call-start = ((), (), s32[]{:S(2)}) async-start(), calls=%async_computation.2 | async-start | bytes 7340032 | tf_op jit(solution)/shard_map/psum | solution.py:31
  96.9 172.2 %all-reduce.11.cloned.1.call-start = ((), (), s32[]{:S(2)}) async-start(), calls=%async_computation.3 | async-start | bytes 4194304 | tf_op jit(solution)/shard_map/psum | solution.py:32
  203.9 114.4 %all-reduce.13.cloned.1.call-start = ((), (), s32[]{:S(2)}) async-start(), calls=%async_computation.4 | async-start | bytes 524288 | tf_op jit(solution)/shard_map/psum | solution.py:34
  275.6 144.2 %all-gather.7.cloned.1.call-start = ((), (), s32[]{:S(2)}) async-start(), calls=%async_computation.8 | async-start | bytes 4587520 | tf_op jit(solution)/shard_map/all_gather | solution.py:54
  277.8 155.2 %all-reduce.15.cloned.1.call-start = ((), (), s32[]{:S(2)}) async-start(), calls=%async_computation.5 | async-start | bytes 524288 | tf_op jit(solution)/shard_map/psum | solution.py:37
  389.9 93.8 %all-gather.5.cloned.1.call-start = ((), (), s32[]{:S(2)}) async-start(), calls=%async_computation.7 | async-start | bytes 4587520 | tf_op jit(solution)/shard_map/all_gather | solution.py:53
  392.1 202.5 %reduce-scatter.2.cloned.1.call-start = ((), (), s32[]{:S(2)}) async-start(), calls=%async_computation.6 | async-start | bytes 13762560 | tf_op jit(solution)/shard_map/reduce_scatter | solution.py:41
  594.6 7.8 %copy-start.1 = (bf16[3584,256]{1,0:T(8,128)(2,1)S(1)}, bf16[3584,256]{1,0:T(8,128)(2,1)}, u32[]{:S(2)}) copy-start(bf16[3584,256]{1,0:T(8,128)(2,1)} %param.7) | copy-start | bytes 5505028
Sparse Core Ops, SparseCore 0:
  17.4 67.8 all-reduce.6
  97.0 95.2 all-reduce.8
  204.1 65.0 all-reduce.10
  275.7 42.6 all-reduce.12
  320.6 48.3 all-gather.6
  390.0 43.0 all-reduce.14
  435.5 48.1 all-gather.4
  486.8 107.7 reduce-scatter.1
where the time goes:
time: 617 us; the launch traced here: 609 us
  waiting for transfers between devices  434 us (70%)
  matrix products  82.4 us (13%)
  other arithmetic  63.6 us (10%)
  between operations  16.6 us (3%)
  local copies, waits for them, and re-layouts  11.9 us (2%)
    reduce_scatter x1, waiting for transfers between devices, local(): lax.psum_scatter(jnp.einsum('kdr,kdc->rkc', projectors, grads, preferred_...  106 us
    psum x1, waiting for transfers between devices, local(): lax.psum(backward_part, 'dp') / columns_total  95.4 us
    psum x1, waiting for transfers between devices, local(): sketched = (lax.psum(sketch_part, 'mp') / rank_total).astype(jnp.bfloat16)  68 us
    psum x1, waiting for transfers between devices, local(): lax.psum(jnp.dot(target, backward, preferred_element_type=jnp.float32), '...  64.7 us
    all_gather x1, waiting for transfers between devices, local(): lax.all_gather(first_own, 'dp', axis=0, tiled=True)  46.3 us
    psum x1, waiting for transfers between devices, local(): gram_full = lax.psum(gram_part, 'dp')  40.5 us
    another operation x6, other arithmetic, local(): factor = jnp.linalg.cholesky(gram_full)  34 us
    dot_general x1, matrix products, local(): jnp.einsum('kdr,kdc->rkc', projectors, grads, preferred_element_type=jnp....  24.7 us
  transfers between devices with their start and end apart: 8, of which 7 were waited for; matrix products, arithmetic and copies ran while one was open for 18% of the time, Pallas kernels for 0%

commit v1 on v0

--- a/solution.py
+++ b/solution.py
@@ -49,8 +49,22 @@
     first_own = lax.dynamic_index_in_dim(first_moment, chosen, 0, keepdims=False)
     second_own = lax.dynamic_index_in_dim(second_moment, chosen, 0, keepdims=False)
     own_start = lax.axis_index("dp") * rank_rows
+
+    def records_treat(packet, along_axis):
+        finding = lax.axis_index(along_axis)
+        taken_in = lax.axis_size(along_axis)
+        later, arr_out, small = (taken_in, finding, packet.shape[0])
+        moved, v1 = (packet, 1)
+        while v1 < later:
+            response = lax.ppermute(
+                moved, axis_name=along_axis, perm=[(dd, (dd - v1) % later) for dd in range(later)]
+            )
+            moved = jnp.concatenate([moved, response], 0)
+            v1 = 2 * v1
+        return jnp.roll(moved, arr_out * small, 0)
+
     first_all, second_all = (
-        lax.all_gather(first_own, "dp", axis=0, tiled=True),
+        records_treat(first_own, "dp"),
         lax.all_gather(second_own, "dp", axis=0, tiled=True),
     )
     own_turning = lax.dynamic_slice_in_dim(turning, own_start, rank_rows, 0)

time: 617 us -> 651 us (1.055)
  waiting for transfers between devices: 434 us -> 455 us
  local copies, waits for them, and re-layouts: 11.9 us -> 20.7 us
    ppermute x0 -> x2, waiting for transfers between devices: none -> 82.2 us  [records_treat(): lax.ppermute(moved, axis_name=along_axis, perm=[(dd, (dd - v1) % later) f...]
    all_gather x1 -> x0, waiting for transfers between devices: 46.3 us -> none  [local(): lax.all_gather(first_own, 'dp', axis=0, tiled=True)]
    psum x1, waiting for transfers between devices: 13.3 us -> 0.01 us  [local(): turning = lax.psum(row_product(new_basis, prior_proj), 'dp')]
    unnamed x4 -> x9, local copies, waits for them, and re-layouts: 0.7 us -> 8.87 us
  transfers between devices with their start and end apart: 8 -> 9, of which waited for: 7 -> 7; matrix products, arithmetic and copies ran while one was open for 18% -> 8% of each run, Pallas kernels for 0% -> 0%
where the time goes in v1:
time: 651 us; the launch traced here: 643 us
  waiting for transfers between devices  455 us (70%)
  matrix products  82.4 us (13%)
  other arithmetic  65 us (10%)
  local copies, waits for them, and re-layouts  20.7 us (3%)
  between operations  16.6 us (3%)
    reduce_scatter x1, waiting for transfers between devices, local(): lax.psum_scatter(jnp.einsum('kdr,kdc->rkc', projectors, grads, preferred_...  102 us
    psum x1, waiting for transfers between devices, local(): lax.psum(backward_part, 'dp') / columns_total  95.4 us
    ppermute x2, waiting for transfers between devices, records_treat(): lax.ppermute(moved, axis_name=along_axis, perm=[(dd, (dd - v1) % later) f...  82.2 us
    psum x1, waiting for transfers between devices, local(): sketched = (lax.psum(sketch_part, 'mp') / rank_total).astype(jnp.bfloat16)  68 us
    psum x1, waiting for transfers between devices, local(): lax.psum(jnp.dot(target, backward, preferred_element_type=jnp.float32), '...  64.7 us
    psum x1, waiting for transfers between devices, local(): gram_full = lax.psum(gram_part, 'dp')  42.7 us
    another operation x6, other arithmetic, local(): factor = jnp.linalg.cholesky(gram_full)  34 us
    dot_general x1, matrix products, local(): jnp.einsum('kdr,kdc->rkc', projectors, grads, preferred_element_type=jnp....  24.7 us
  transfers between devices with their start and end apart: 9, of which 7 were waited for; matrix products, arithmetic and copies ran while one was open for 8% of the time, Pallas kernels for 0%

profile of v1, /device:TPU:0, one launch (start us, length us, event | category | flops | bytes accessed | tf_op | source)
XLA Modules:
  0.0 643.4 jit_solution(11607018151543322104)
XLA Ops:
  8.7 8.6 %fusion.4 = f32[2048,256]{1,0:T(8,128)} fusion(bf16[3584,256]{1,0:T(8,128)(2,1)S(1)} %copy-done, bf16[3,2048,3584]{2,1,0:T(8,128)(2,1)} %param.6, s32[]{:T(128)S(6)} %select_n.40), kind=kOutput, calls=%fused_computation.6 | convolution fusion | flops 3758096384 | bytes 18612228 | tf_op jit(solution)/shard_map/dot_general | solution.py:26
  17.3 68.0 %all-reduce.7.cloned.1.call-done = f32[2048,256]{1,0:T(8,128)} async-done(((f32[2048,256]{1,0:T(8,128)}), f32[2048,256]{1,0:T(8,128)}) %all-reduce.7.cloned.1.call-update) | async-done | bytes 2097168 | tf_op jit(solution)/shard_map/psum | solution.py:27
  85.3 11.6 %fusion.2 = f32[3584,256]{1,0:T(8,128)} fusion(bf16[3,2048,3584]{2,1,0:T(8,128)(2,1)} %param.6, s32[]{:T(128)S(6)} %select_n.40, f32[2048,256]{1,0:T(8,128)} %all-reduce.7.cloned.1.call-done), kind=kOutput, calls=%fused_computation.4 | convolution fusion | flops 3759144960 | bytes 20447236 | tf_op jit(solution)/shard_map/dot_general | solution.py:28
  97.0 95.4 %all-reduce.9.cloned.1.call-done = f32[3584,256]{1,0:T(8,128)} async-done(((f32[3584,256]{1,0:T(8,128)}), f32[3584,256]{1,0:T(8,128)}) %all-reduce.9.cloned.1.call-update) | async-done | bytes 3670032 | tf_op jit(solution)/shard_map/psum | solution.py:31
  192.4 11.5 %fusion = f32[2048,256]{1,0:T(8,128)} fusion(bf16[3,2048,3584]{2,1,0:T(8,128)(2,1)} %param.6, s32[]{:T(128)S(6)} %select_n.40, f32[3584,256]{1,0:T(8,128)} %all-reduce.9.cloned.1.call-done), kind=kOutput, calls=%fused_computation.2 | convolution fusion | flops 3759931392 | bytes 20447236 | tf_op jit(solution)/shard_map/dot_general | solution.py:32
  204.4 64.7 %all-reduce.11.cloned.1.call-done = f32[2048,256]{1,0:T(8,128)} async-done(((f32[2048,256]{1,0:T(8,128)}), f32[2048,256]{1,0:T(8,128)}) %all-reduce.11.cloned.1.call-update) | async-done | bytes 2097168 | tf_op jit(solution)/shard_map/psum | solution.py:32
  269.2 6.4 fusion.48
  275.6 42.7 %all-reduce.13.cloned.1.call-done = f32[256,256]{0,1:T(8,128)} async-done(((f32[256,256]{0,1:T(8,128)}), f32[256,256]{0,1:T(8,128)}) %all-reduce.13.cloned.1.call-update) | async-done | bytes 262160 | tf_op jit(solution)/shard_map/psum | solution.py:34
  320.5 11.7 %cholesky.50 = f32[128,128]{1,0:T(8,128)S(1)} custom-call(f32[128,128]{1,0:T(8,128)S(1)} %cholesky.118), custom_call_target="Cholesky" | custom-call | tf_op jit(solution)/shard_map/jit(cholesky)/cholesky | solution.py:35
  332.2 9.8 %custom-call.15 = f32[1,128,128]{1,2,0:T(8,128)S(1)} custom-call(f32[1,128,128]{2,1,0:T(8,128)S(1)} %get-tuple-element.29), custom_call_target="InvertDiagBlocksLowerTriangular" | custom-call | tf_op jit(solution)/shard_map/jit(cholesky)/cholesky | solution.py:35
  342.5 11.7 %cholesky.105 = f32[128,128]{1,0:T(8,128)S(1)} custom-call(f32[128,128]{1,0:T(8,128)S(1)} %convolution_subtract_fusion.1), custom_call_target="Cholesky" | custom-call | tf_op jit(solution)/shard_map/jit(cholesky)/cholesky | solution.py:35
  356.3 4.2 while.1
  357.1 1.4 bitcast_dynamic-update-slice_fusion.2
  359.1 1.4 bitcast_dynamic-update-slice_fusion.2
  360.5 19.7 %custom-call.16 = f32[2,128,128]{1,2,0:T(8,128)S(1)} custom-call(f32[2,128,128]{2,1,0:T(8,128)S(1)} %get-tuple-element.10), custom_call_target="InvertDiagBlocksLowerTriangular" | custom-call | tf_op jit(solution)/shard_map/jit(_solve_triangular)/triangular_solve | solution.py:36
  380.2 2.3 fusion.22
  382.5 3.0 convolution_subtract_fusion
  386.6 3.0 fusion.19
  389.7 2.2 constant_dynamic-slice_fusion.1
  393.1 1.7 copy.11
  394.7 24.7 %convolution_bitcast_fusion = f32[256,3,3584]{2,0,1:T(8,128)} fusion(bf16[3,2048,3584]{2,1,0:T(8,128)(2,1)} %param.6, bf16[3,2048,256]{2,1,0:T(8,128)(2,1)} %param.8, pred[3]{0:T(512)(128)(4,1)S(1)} %iota_compare_fusion.3, bf16[2048,256]{1,0:T(8,128)(2,1)S(1)} %copy.11), kind=kOutput, calls=%fused_computation.11 | convolution fusion | flops 11275862016 | bytes 59244548 | tf_op jit(solution)/shard_map/kdr,kdc->rkc/dot_general | solution.py:42
  419.5 2.3 constant_dynamic-update-slice_fusion.5
  421.8 1.5 collective-permute-start
  423.3 21.5 %collective-permute-done = f32[64,3584]{1,0:T(8,128)S(1)} collective-permute-done((f32[64,3584]{1,0:T(8,128)S(1)}, f32[64,3584]{1,0:T(8,128)S(1)}, u32[]{:S(2)}, u32[]{:S(2)}) %collective-permute-start) | collective-permute-done | bytes 917536 | tf_op jit(solution)/shard_map/ppermute | solution.py:59
  446.2 1.4 collective-permute-start.1
  448.6 60.6 %collective-permute-done.1 = f32[128,3584]{1,0:T(8,128)} collective-permute-done((f32[128,3584]{1,0:T(8,128)}, f32[128,3584]{1,0:T(8,128)}, u32[]{:S(2)}, u32[]{:S(2)}) %collective-permute-start.1) | collective-permute-done | bytes 1835040 | tf_op jit(solution)/shard_map/ppermute | solution.py:59
  509.2 2.9 constant_dynamic-update-slice_fusion.3
  514.0 2.9 constant_dynamic-update-slice_fusion
  516.9 4.4 fusion.11
  521.3 5.3 fusion.9
  526.7 101.8 %reduce-scatter.2.cloned.1.call-done = f32[64,3,3584]{2,0,1:T(8,128)} async-done(((f32[256,3,3584]{2,0,1:T(8,128)}), f32[64,3,3584]{2,0,1:T(8,128)}) %reduce-scatter.2.cloned.1.call-update) | async-done | bytes 2752528 | tf_op jit(solution)/shard_map/reduce_scatter | solution.py:41
  628.5 7.9 %divide_convert_fusion = (bf16[3,64,3584]{2,1,0:T(8,128)(2,1)}, f32[3,64,3584]{2,1,0:T(8,128)}, f32[3,64,3584]{2,1,0:T(8,128)}) fusion(f32[64,3,3584]{2,0,1:T(8,128)} %reduce-scatter.2.cloned.1.call-done, f32[3,64,3584]{2,1,0:T(8,128)} %param.10, f32[64,3584]{1,0:T(8,128)} %fusion.9, pred[3]{0:T(512)(128)(4,1)S(1)} %iota_compare_fusion.3, ...), kind=kLoop, calls=%fused_computation.23 | loop fusion | flops 8257536 | bytes 16973828 | tf_op jit(solution)/shard_map/convert_element_type | solution.py:77
  (44 shorter events, 12.7 us)
Async XLA Ops:
  7.2 1.5 copy-start
  7.2 78.1 %all-reduce.7.cloned.1.call-start = ((), (), s32[]{:S(2)}) async-start(), calls=%async_computation.1 | async-start | bytes 4194304 | tf_op jit(solution)/shard_map/psum | solution.py:27
  17.3 175.1 %all-reduce.9.cloned.1.call-start = ((), (), s32[]{:S(2)}) async-start(), calls=%async_computation.2 | async-start | bytes 7340032 | tf_op jit(solution)/shard_map/psum | solution.py:31
  96.9 172.2 %all-reduce.11.cloned.1.call-start = ((), (), s32[]{:S(2)}) async-start(), calls=%async_computation.3 | async-start | bytes 4194304 | tf_op jit(solution)/shard_map/psum | solution.py:32
  203.9 114.4 %all-reduce.13.cloned.1.call-start = ((), (), s32[]{:S(2)}) async-start(), calls=%async_computation.4 | async-start | bytes 524288 | tf_op jit(solution)/shard_map/psum | solution.py:34
  275.6 241.4 %all-reduce.15.cloned.1.call-start = ((), (), s32[]{:S(2)}) async-start(), calls=%async_computation.5 | async-start | bytes 524288 | tf_op jit(solution)/shard_map/psum | solution.py:37
  389.6 131.7 %all-gather.3.cloned.1.call-start = ((), (), s32[]{:S(2)}) async-start(), calls=%async_computation.7 | async-start | bytes 4587520 | tf_op jit(solution)/shard_map/all_gather | solution.py:68
  391.9 236.6 %reduce-scatter.2.cloned.1.call-start = ((), (), s32[]{:S(2)}) async-start(), calls=%async_computation.6 | async-start | bytes 13762560 | tf_op jit(solution)/shard_map/reduce_scatter | solution.py:41
  421.8 23.0 %collective-permute-start = (f32[64,3584]{1,0:T(8,128)S(1)}, f32[64,3584]{1,0:T(8,128)S(1)}, u32[]{:S(2)}, u32[]{:S(2)}) collective-permute-start(f32[64,3584]{1,0:T(8,128)S(1)} %get-tuple-element.23), channel_id=1, source_target_pairs={{0,24},{8,0},{16,8},{24,16},{1,25},{9,1},{17,9},{25,17},{2,26},{10... | collective-permute-start | bytes 2752520 | tf_op jit(solution)/shard_map/ppermute | solution.py:59
  446.2 63.0 %collective-permute-start.1 = (f32[128,3584]{1,0:T(8,128)}, f32[128,3584]{1,0:T(8,128)}, u32[]{:S(2)}, u32[]{:S(2)}) collective-permute-start(f32[128,3584]{1,0:T(8,128)} %pad_maximum_fusion.1), channel_id=1, source_target_pairs={{0,16},{8,24},{16,0},{24,8},{1,17},{9,25},{17,1},{25,9},{2,18},{10... | collective-permute-start | bytes 5505032 | tf_op jit(solution)/shard_map/ppermute | solution.py:59
  628.5 7.9 %copy-start.1 = (bf16[3584,256]{1,0:T(8,128)(2,1)S(1)}, bf16[3584,256]{1,0:T(8,128)(2,1)}, u32[]{:S(2)}) copy-start(bf16[3584,256]{1,0:T(8,128)(2,1)} %param.7) | copy-start | bytes 5505028
Sparse Core Ops, SparseCore 0:
  17.4 67.8 all-reduce.6
  97.0 95.2 all-reduce.8
  204.1 65.0 all-reduce.10
  275.7 42.6 all-reduce.12
  389.8 43.2 all-reduce.14
  435.3 81.2 all-gather.2
  519.7 108.6 reduce-scatter.1
